TPU v7x, 32 devices: a whole 2x2x4 slice. The times are simulated.
32 devices in a mesh: term: 4 (over y, x), sector: 8 (over z, core).
Axes of the slice: x: 2, y: 2, z: 4, core: 2. Of those that a mesh axis runs over, the one named last changes fastest.
Arguments:
- psi: bfloat16 [8, 8, 128, 128], P('sector'), may hold values from -6 to 6
- left_env: bfloat16 [8, 8, 128, 128], P('term', 'sector'), may hold values from -40 to 40
- right_env: bfloat16 [8, 8, 128, 128], P('term', 'sector'), may hold values from -4 to 4
- precond: bfloat16 [8, 8, 128, 128], P('sector'), may hold values from 0.5 to 4
- block_sizes: int32 [8], replicated, may hold values from 32 to 128, as said below
Outputs:
- state: bfloat16 [8, 8, 128, 128], P('sector')
- energy: float32 [3], replicated
Inputs may be any that keep to these rules, and one draw needn't show every extreme that they name: `block_sizes`: some sector has exactly 128 rows in every draw.
All inputs are finite; a program needn't handle non-finite values.
Results may differ from a plain program's by a relative error of at most 0.022.
Values may be sent and summed in bfloat16 or wider, within the bound.
No kernel may reach another device: no remote copies, remote signals or barrier semaphores. Data moves between devices by JAX's collectives and lax.ppermute only.
A program may use at most 128 MiB of HBM per device.

v0:
```python
import jax
import jax.numpy as jnp
from jax import lax
from jax.sharding import PartitionSpec as P

ITERS = 3


def block_mask(block_sizes, width, own_row):
    rows = jnp.arange(width)
    valid = rows[None, :] < block_sizes[:, None]
    own_valid = lax.dynamic_slice_in_dim(valid, own_row, 1, 0)[0]
    return (own_valid[None, :, None] & valid[:, None, :]).astype(jnp.float32)


def dot_sums(cur_share, img_share, pre_share, count):
    first = lax.psum(
        (jnp.sum(cur_share * cur_share), jnp.sum(cur_share * img_share)), ("term", "sector")
    )
    theta = first[1] / first[0]
    fresh = cur_share - (img_share - theta * cur_share) / pre_share
    squares = lax.psum(jnp.sum(fresh * fresh), ("term", "sector"))
    return (theta, lax.rsqrt(squares / count + 1e-06))


def local(psi, left_env, right_env, precond, block_sizes):
    sectors = block_sizes.shape[0]
    width = psi.shape[-1]
    own_row = lax.axis_index("sector")
    share = sectors // lax.axis_size("term")
    share_start = lax.axis_index("term") * share
    count = float(sectors * sectors * width * width)
    mask = block_mask(block_sizes, width, own_row)
    state = (psi[0].astype(jnp.float32) * mask).astype(jnp.bfloat16)
    scaling = precond[0].astype(jnp.float32)
    left_own = left_env[:, 0]

    def portion(values):
        return lax.dynamic_slice_in_dim(values, share_start, share, 0)

    right_all = lax.all_gather(right_env, "sector", axis=1, tiled=True)
    energies = []
    for step in range(ITERS):
        images = jnp.einsum(
            "jab,kjcb->kjac", state, right_all, preferred_element_type=jnp.float32
        ).astype(jnp.bfloat16)
        partial_value = jnp.einsum(
            "kac,kjcd->jad", left_own, images, preferred_element_type=jnp.float32
        )
        current = state.astype(jnp.float32)
        image = lax.psum(partial_value.astype(jnp.bfloat16), "term").astype(jnp.float32) * mask
        theta, factor = dot_sums(portion(current), portion(image), portion(scaling), count)
        fresh = current - (image - theta * current) / scaling
        state = (fresh * factor).astype(jnp.bfloat16)
        energies.append(theta)
    return (state[None], jnp.stack(energies))


def solution(mesh):
    in_specs = (
        P("sector", None, None, None),
        P("term", "sector", None, None),
        P("term", "sector", None, None),
        P("sector", None, None, None),
        P(),
    )
    out_specs = (P("sector", None, None, None), P())
    return jax.shard_map(local, mesh=mesh, in_specs=in_specs, out_specs=out_specs, check_vma=False)
```

profile of v0, /device:TPU:0, one launch (start us, length us, event | category | flops | bytes accessed | tf_op | source)
XLA Modules:
  0.0 424.9 jit_solution(16946019127858269423)
XLA Ops:
  7.2 0.6 copy-done.6
  7.9 0.1 iota_compare_fusion
  8.0 1.1 copy.7
  9.1 16.6 %all_gather.3 = bf16[2,8,128,128]{3,2,1,0:T(8,128)(2,1)S(1)} all-gather(bf16[2,1,128,128]{3,2,1,0:T(8,128)(2,1)S(1)} %copy-done.5), channel_id=1, replica_groups=mesh['term'=4,'sector'=8] {'sector'}, dimensions={1}, use_global_device_ids=true | all-gather | bytes 589824 | tf_op jit(solution)/shard_map/all_gather | solution.py:41
  25.7 1.2 fusion.8
  27.1 0.9 copy-done.4
  27.9 0.2 copy.8
  28.1 43.0 %all-reduce.7.cloned.1.call-done = bf16[8,128,128]{1,2,0:T(8,128)(2,1)} async-done(((bf16[8,128,128]{1,2,0:T(8,128)(2,1)}), bf16[8,128,128]{1,2,0:T(8,128)(2,1)}) %all-reduce.7.cloned.1.call-update) | async-done | bytes 262160 | tf_op jit(solution)/shard_map/psum | solution.py:51
  71.1 1.2 fusion.34
  72.3 0.6 multiply_reduce_fusion.4
  72.9 39.6 %all-reduce.2 = (f32[]{:T(128)}, f32[]{:T(128)}) all-reduce(f32[]{:T(128)} %get-tuple-element.9, f32[]{:T(128)} %get-tuple-element.8), channel_id=1, replica_groups=mesh['term'=4,'sector'=8] {'term','sector'}, use_global_device_ids=true, to_apply=%region_2.0 | all-reduce | flops 2 | bytes 16 | tf_op jit(solution)/shard_map/psum | solution.py:17
  113.9 0.7 fusion.43
  114.5 41.4 %psum.87 = f32[]{:T(128)} all-reduce(f32[]{:T(128)} %fusion.43), channel_id=1, replica_groups=mesh['term'=4,'sector'=8] {'term','sector'}, use_global_device_ids=true, to_apply=%region_6.0 | all-reduce | flops 1 | bytes 8 | tf_op jit(solution)/shard_map/psum | solution.py:22
  156.6 0.3 fusion.52
  156.9 1.2 fusion.7
  158.1 43.0 %all-reduce.9.cloned.1.call-done = bf16[8,128,128]{1,2,0:T(8,128)(2,1)} async-done(((bf16[8,128,128]{1,2,0:T(8,128)(2,1)}), bf16[8,128,128]{1,2,0:T(8,128)(2,1)}) %all-reduce.9.cloned.1.call-update) | async-done | bytes 262160 | tf_op jit(solution)/shard_map/psum | solution.py:51
  201.2 1.1 and_select_fusion.1
  202.3 0.6 multiply_reduce_fusion.2
  203.0 39.6 %all-reduce.1 = (f32[]{:T(128)}, f32[]{:T(128)}) all-reduce(f32[]{:T(128)} %get-tuple-element.7, f32[]{:T(128)} %get-tuple-element.6), channel_id=1, replica_groups=mesh['term'=4,'sector'=8] {'term','sector'}, use_global_device_ids=true, to_apply=%region_9.0 | all-reduce | flops 2 | bytes 16 | tf_op jit(solution)/shard_map/psum | solution.py:17
  243.9 0.7 fusion.42
  244.5 41.4 %psum.91 = f32[]{:T(128)} all-reduce(f32[]{:T(128)} %fusion.42), channel_id=1, replica_groups=mesh['term'=4,'sector'=8] {'term','sector'}, use_global_device_ids=true, to_apply=%region_13.0 | all-reduce | flops 1 | bytes 8 | tf_op jit(solution)/shard_map/psum | solution.py:22
  286.6 0.3 fusion.50
  286.9 1.2 fusion.6
  288.1 43.1 %all-reduce.11.cloned.1.call-done = bf16[8,128,128]{1,2,0:T(8,128)(2,1)} async-done(((bf16[8,128,128]{1,2,0:T(8,128)(2,1)}), bf16[8,128,128]{1,2,0:T(8,128)(2,1)}) %all-reduce.11.cloned.1.call-update) | async-done | bytes 262160 | tf_op jit(solution)/shard_map/psum | solution.py:51
  331.2 1.1 and_select_fusion
  332.3 0.6 multiply_reduce_fusion
  333.0 39.6 %all-reduce = (f32[]{:T(128)}, f32[]{:T(128)}) all-reduce(f32[]{:T(128)} %get-tuple-element.5, f32[]{:T(128)} %get-tuple-element.4), channel_id=1, replica_groups=mesh['term'=4,'sector'=8] {'term','sector'}, use_global_device_ids=true, to_apply=%region_16.0 | all-reduce | flops 2 | bytes 16 | tf_op jit(solution)/shard_map/psum | solution.py:17
  373.9 0.7 fusion.41
  374.5 41.4 %psum.95 = f32[]{:T(128)} all-reduce(f32[]{:T(128)} %fusion.41), channel_id=1, replica_groups=mesh['term'=4,'sector'=8] {'term','sector'}, use_global_device_ids=true, to_apply=%region_20.0 | all-reduce | flops 1 | bytes 8 | tf_op jit(solution)/shard_map/psum | solution.py:22
  416.6 0.3 fusion.31
  416.9 0.9 copy.9
  417.7 0.6 pad_maximum_fusion
  (20 shorter events, 0.2 us)
Async XLA Ops:
  7.2 18.6 %copy-start = (bf16[2,1,128,128]{3,2,1,0:T(8,128)(2,1)S(1)}, bf16[2,1,128,128]{3,2,1,0:T(8,128)(2,1)}, u32[]{:S(2)}) copy-start(bf16[2,1,128,128]{3,2,1,0:T(8,128)(2,1)} %param.6) | copy-start | bytes 196612
  7.2 64.0 %all-reduce.7.cloned.1.call-start = ((), (), s32[]{:S(2)}) async-start(), calls=%async_computation | async-start | bytes 524288 | tf_op jit(solution)/shard_map/psum | solution.py:51
  7.2 0.7 copy-start.6
  8.0 1.2 copy-start.5
  27.0 0.9 copy-start.4
  27.0 174.2 %all-reduce.9.cloned.1.call-start = ((), (), s32[]{:S(2)}) async-start(), calls=%async_computation.1 | async-start | bytes 524288 | tf_op jit(solution)/shard_map/psum | solution.py:51
  72.9 83.6 %copy-start.1 = (bf16[8,128,128]{1,2,0:T(8,128)(2,1)S(1)}, bf16[8,128,128]{1,2,0:T(8,128)(2,1)}, u32[]{:S(2)}) copy-start(bf16[8,128,128]{1,2,0:T(8,128)(2,1)} %all-reduce.7.cloned.1.call-done) | copy-start | bytes 786436
  158.1 173.1 %all-reduce.11.cloned.1.call-start = ((), (), s32[]{:S(2)}) async-start(), calls=%async_computation.2 | async-start | bytes 524288 | tf_op jit(solution)/shard_map/psum | solution.py:51
  203.0 83.6 %copy-start.3 = (bf16[8,128,128]{1,2,0:T(8,128)(2,1)S(1)}, bf16[8,128,128]{1,2,0:T(8,128)(2,1)}, u32[]{:S(2)}) copy-start(bf16[8,128,128]{1,2,0:T(8,128)(2,1)} %all-reduce.9.cloned.1.call-done) | copy-start | bytes 786436
  333.0 83.6 %copy-start.2 = (bf16[8,128,128]{1,2,0:T(8,128)(2,1)S(1)}, bf16[8,128,128]{1,2,0:T(8,128)(2,1)}, u32[]{:S(2)}) copy-start(bf16[8,128,128]{1,2,0:T(8,128)(2,1)} %all-reduce.11.cloned.1.call-done) | copy-start | bytes 786436
Sparse Core Ops, SparseCore 0:
  27.1 43.9 all-reduce.6
  158.2 42.9 all-reduce.8
  288.2 42.9 all-reduce.10
where the time goes:
time: 426 us; the launch traced here: 425 us
  blocking collectives  259 us (61%)
  waiting for transfers between devices  129 us (30%)
  between operations  20 us (5%)
  other arithmetic  8.96 us (2%)
    psum x3, waiting for transfers between devices, local(): lax.psum(partial_value.astype(jnp.bfloat16), 'term').astype(jnp.float32)  129 us
    psum x3, blocking collectives, dot_sums(): squares = lax.psum(jnp.sum(fresh * fresh), ('term', 'sector'))  124 us
    psum x3, blocking collectives, dot_sums(): lax.psum((jnp.sum(cur_share * cur_share), jnp.sum(cur_share * img_share))...  119 us
    all_gather x1, blocking collectives, local(): right_all = lax.all_gather(right_env, 'sector', axis=1, tiled=True)  16.6 us
  transfers between devices with their start and end apart: 3, of which 3 were waited for; matrix products, arithmetic and copies ran while one was open for 0% of the time, Pallas kernels for 0%

commit v1 on v0

--- a/solution.py
+++ b/solution.py
@@ -4,6 +4,22 @@
 from jax.sharding import PartitionSpec as P
 
 ITERS = 3
+
+
+def collect(x, axis, dim):
+    ways, here, step = (lax.axis_size(axis), lax.axis_index(axis), x.shape[dim])
+    dims = [n * ways if d == dim else n for d, n in enumerate(x.shape)]
+    full = lax.dynamic_update_slice_in_dim(jnp.zeros(dims, x.dtype), x, here * step, axis=dim)
+    going_up = going_down = x
+    for far in range(1, ways // 2 + 1):
+        going_up = lax.ppermute(going_up, axis, [(d, (d + 1) % ways) for d in range(ways)])
+        full = lax.dynamic_update_slice_in_dim(full, going_up, (here - far) % ways * step, axis=dim)
+        if 2 * far < ways:
+            going_down = lax.ppermute(going_down, axis, [(d, (d - 1) % ways) for d in range(ways)])
+            full = lax.dynamic_update_slice_in_dim(
+                full, going_down, (here + far) % ways * step, axis=dim
+            )
+    return full
 
 
 def block_mask(block_sizes, width, own_row):
@@ -38,7 +54,7 @@
     def portion(values):
         return lax.dynamic_slice_in_dim(values, share_start, share, 0)
 
-    right_all = lax.all_gather(right_env, "sector", axis=1, tiled=True)
+    right_all = collect(right_env, "sector", 1)
     energies = []
     for step in range(ITERS):
         images = jnp.einsum(

time: 426 us -> 433 us (1.016)
  blocking collectives: 259 us -> 243 us
  starting transfers between devices: 0.12 us -> 12 us
  waiting for transfers between devices: 129 us -> 139 us
    all_gather x1 -> x0, blocking collectives: 16.6 us -> none  [local(): right_all = lax.all_gather(right_env, 'sector', axis=1, tiled=True)]
    ppermute x0 -> x7, waiting for transfers between devices: none -> 12.8 us  [the longest x4 10.9 us: collect(): lax.ppermute(going_up, axis, [(d, (d + 1) % ways) for d in range(ways)])]
    ppermute x0 -> x7, starting transfers between devices: none -> 11.8 us  [the longest x3 11.8 us: collect(): lax.ppermute(going_down, axis, [(d, (d - 1) % ways) for d in range(ways)])]
  transfers between devices with their start and end apart: 3 -> 10, of which waited for: 3 -> 6; matrix products, arithmetic and copies ran while one was open for 0% -> 0% of each run, Pallas kernels for 0% -> 0%
where the time goes in v1:
time: 433 us; the launch traced here: 431 us
  blocking collectives  243 us (56%)
  waiting for transfers between devices  139 us (32%)
  between operations  20.1 us (5%)
  starting transfers between devices  12 us (3%)
  other arithmetic  8.96 us (2%)
  local copies, waits for them, and re-layouts  4.65 us (1%)
    psum x3, waiting for transfers between devices, local(): lax.psum(partial_value.astype(jnp.bfloat16), 'term').astype(jnp.float32)  126 us
    psum x3, blocking collectives, dot_sums(): squares = lax.psum(jnp.sum(fresh * fresh), ('term', 'sector'))  124 us
    psum x3, blocking collectives, dot_sums(): lax.psum((jnp.sum(cur_share * cur_share), jnp.sum(cur_share * img_share))...  119 us
    ppermute x3, starting transfers between devices, collect(): lax.ppermute(going_down, axis, [(d, (d - 1) % ways) for d in range(ways)])  11.8 us
    ppermute x4, waiting for transfers between devices, collect(): lax.ppermute(going_up, axis, [(d, (d + 1) % ways) for d in range(ways)])  10.9 us
  transfers between devices with their start and end apart: 10, of which 6 were waited for; matrix products, arithmetic and copies ran while one was open for 0% of the time, Pallas kernels for 0%

profile of v1, /device:TPU:0, one launch (start us, length us, event | category | flops | bytes accessed | tf_op | source)
XLA Modules:
  0.0 431.2 jit_solution(1075891830632880875)
XLA Ops:
  7.2 4.5 %collective-permute-start.1 = (bf16[2,1,128,128]{3,2,1,0:T(8,128)(2,1)}, bf16[2,1,128,128]{3,2,1,0:T(8,128)(2,1)S(1)}, u32[]{:S(2)}, u32[]{:S(2)}) collective-permute-start(bf16[2,1,128,128]{3,2,1,0:T(8,128)(2,1)} %param.7), channel_id=1, source_target_pairs={{0,7},{1,0},{2,1},{3,2},{4,3},{5,4},{6,5},{7,6},{8,15},{9,8},{10,9... | collective-permute-start | bytes 196616 | tf_op jit(solution)/shard_map/ppermute | solution.py:18
  11.8 0.7 copy-done.6
  12.5 1.1 copy.7
  13.8 0.7 copy-done.5
  14.5 3.6 collective-permute-start.3
  18.2 1.9 collective-permute-done.3
  20.0 3.7 collective-permute-start.5
  23.8 5.4 %collective-permute-done.4 = bf16[2,1,128,128]{3,2,1,0:T(8,128)(2,1)S(1)} collective-permute-done((bf16[2,1,128,128]{3,2,1,0:T(8,128)(2,1)S(1)}, bf16[2,1,128,128]{3,2,1,0:T(8,128)(2,1)S(1)}, u32[]{:S(2)}, u32[]{:S(2)}) %collective-permute-start.4) | collective-permute-done | bytes 65568 | tf_op jit(solution)/shard_map/ppermute | solution.py:15
  29.3 5.4 %collective-permute-done.6 = bf16[2,1,128,128]{3,2,1,0:T(8,128)(2,1)S(1)} collective-permute-done((bf16[2,1,128,128]{3,2,1,0:T(8,128)(2,1)S(1)}, bf16[2,1,128,128]{3,2,1,0:T(8,128)(2,1)S(1)}, u32[]{:S(2)}, u32[]{:S(2)}) %collective-permute-start.6) | collective-permute-done | bytes 65568 | tf_op jit(solution)/shard_map/ppermute | solution.py:15
  34.8 1.3 fusion.8
  36.1 0.9 copy-done.4
  37.2 40.1 %all-reduce.7.cloned.1.call-done = bf16[8,128,128]{1,2,0:T(8,128)(2,1)} async-done(((bf16[8,128,128]{1,2,0:T(8,128)(2,1)}), bf16[8,128,128]{1,2,0:T(8,128)(2,1)}) %all-reduce.7.cloned.1.call-update) | async-done | bytes 262160 | tf_op jit(solution)/shard_map/psum | solution.py:67
  77.4 1.2 fusion.34
  78.5 0.6 multiply_reduce_fusion.4
  79.2 39.6 %all-reduce.2 = (f32[]{:T(128)}, f32[]{:T(128)}) all-reduce(f32[]{:T(128)} %get-tuple-element.9, f32[]{:T(128)} %get-tuple-element.8), channel_id=1, replica_groups=mesh['term'=4,'sector'=8] {'term','sector'}, use_global_device_ids=true, to_apply=%region_2.3 | all-reduce | flops 2 | bytes 16 | tf_op jit(solution)/shard_map/psum | solution.py:33
  120.1 0.7 fusion.43
  120.8 41.4 %psum.87 = f32[]{:T(128)} all-reduce(f32[]{:T(128)} %fusion.43), channel_id=1, replica_groups=mesh['term'=4,'sector'=8] {'term','sector'}, use_global_device_ids=true, to_apply=%region_6.7 | all-reduce | flops 1 | bytes 8 | tf_op jit(solution)/shard_map/psum | solution.py:38
  163.1 1.2 fusion.7
  164.4 43.0 %all-reduce.9.cloned.1.call-done = bf16[8,128,128]{1,2,0:T(8,128)(2,1)} async-done(((bf16[8,128,128]{1,2,0:T(8,128)(2,1)}), bf16[8,128,128]{1,2,0:T(8,128)(2,1)}) %all-reduce.9.cloned.1.call-update) | async-done | bytes 262160 | tf_op jit(solution)/shard_map/psum | solution.py:67
  207.4 1.1 and_select_fusion.1
  208.6 0.6 multiply_reduce_fusion.2
  209.2 39.6 %all-reduce.1 = (f32[]{:T(128)}, f32[]{:T(128)}) all-reduce(f32[]{:T(128)} %get-tuple-element.7, f32[]{:T(128)} %get-tuple-element.6), channel_id=1, replica_groups=mesh['term'=4,'sector'=8] {'term','sector'}, use_global_device_ids=true, to_apply=%region_9.10 | all-reduce | flops 2 | bytes 16 | tf_op jit(solution)/shard_map/psum | solution.py:33
  250.1 0.7 fusion.42
  250.8 41.4 %psum.91 = f32[]{:T(128)} all-reduce(f32[]{:T(128)} %fusion.42), channel_id=1, replica_groups=mesh['term'=4,'sector'=8] {'term','sector'}, use_global_device_ids=true, to_apply=%region_13.14 | all-reduce | flops 1 | bytes 8 | tf_op jit(solution)/shard_map/psum | solution.py:38
  293.2 1.2 fusion.6
  294.4 43.1 %all-reduce.11.cloned.1.call-done = bf16[8,128,128]{1,2,0:T(8,128)(2,1)} async-done(((bf16[8,128,128]{1,2,0:T(8,128)(2,1)}), bf16[8,128,128]{1,2,0:T(8,128)(2,1)}) %all-reduce.11.cloned.1.call-update) | async-done | bytes 262160 | tf_op jit(solution)/shard_map/psum | solution.py:67
  337.5 1.1 and_select_fusion
  338.6 0.6 multiply_reduce_fusion
  339.3 39.6 %all-reduce = (f32[]{:T(128)}, f32[]{:T(128)}) all-reduce(f32[]{:T(128)} %get-tuple-element.5, f32[]{:T(128)} %get-tuple-element.4), channel_id=1, replica_groups=mesh['term'=4,'sector'=8] {'term','sector'}, use_global_device_ids=true, to_apply=%region_16.17 | all-reduce | flops 2 | bytes 16 | tf_op jit(solution)/shard_map/psum | solution.py:33
  380.2 0.7 fusion.41
  380.9 41.4 %psum.95 = f32[]{:T(128)} all-reduce(f32[]{:T(128)} %fusion.41), channel_id=1, replica_groups=mesh['term'=4,'sector'=8] {'term','sector'}, use_global_device_ids=true, to_apply=%region_20.21 | all-reduce | flops 1 | bytes 8 | tf_op jit(solution)/shard_map/psum | solution.py:38
  423.2 0.9 copy.9
  (42 shorter events, 2.3 us)
Async XLA Ops:
  7.2 27.6 %copy-start = (bf16[2,1,128,128]{3,2,1,0:T(8,128)(2,1)S(1)}, bf16[2,1,128,128]{3,2,1,0:T(8,128)(2,1)}, u32[]{:S(2)}) copy-start(bf16[2,1,128,128]{3,2,1,0:T(8,128)(2,1)} %param.6) | copy-start | bytes 196612
  7.2 70.2 %all-reduce.7.cloned.1.call-start = ((), (), s32[]{:S(2)}) async-start(), calls=%async_computation | async-start | bytes 524288 | tf_op jit(solution)/shard_map/psum | solution.py:67
  7.2 7.3 %collective-permute-start.1 = (bf16[2,1,128,128]{3,2,1,0:T(8,128)(2,1)}, bf16[2,1,128,128]{3,2,1,0:T(8,128)(2,1)S(1)}, u32[]{:S(2)}, u32[]{:S(2)}) collective-permute-start(bf16[2,1,128,128]{3,2,1,0:T(8,128)(2,1)} %param.7), channel_id=1, source_target_pairs={{0,7},{1,0},{2,1},{3,2},{4,3},{5,4},{6,5},{7,6},{8,15},{9,8},{10,9... | collective-permute-start | bytes 196616 | tf_op jit(solution)/shard_map/ppermute | solution.py:18
  11.8 6.4 %collective-permute-start = (bf16[2,1,128,128]{3,2,1,0:T(8,128)(2,1)}, bf16[2,1,128,128]{3,2,1,0:T(8,128)(2,1)S(1)}, u32[]{:S(2)}, u32[]{:S(2)}) collective-permute-start(bf16[2,1,128,128]{3,2,1,0:T(8,128)(2,1)} %param.7), channel_id=1, source_target_pairs={{0,1},{1,2},{2,3},{3,4},{4,5},{5,6},{6,7},{7,0},{8,9},{9,10},{10,1... | collective-permute-start | bytes 196616 | tf_op jit(solution)/shard_map/ppermute | solution.py:15
  11.8 0.7 copy-start.6
  13.7 0.8 copy-start.5
  14.5 5.5 %collective-permute-start.3 = (bf16[2,1,128,128]{3,2,1,0:T(8,128)(2,1)S(1)}, bf16[2,1,128,128]{3,2,1,0:T(8,128)(2,1)S(1)}, u32[]{:S(2)}, u32[]{:S(2)}) collective-permute-start(bf16[2,1,128,128]{3,2,1,0:T(8,128)(2,1)S(1)} %collective-permute-done.1), channel_id=1, source_target_pairs={{0,7},{1,0},{2,1},{3,2},{4,3},{5,4},{6,5},{7,6},{8,15},{9,8},{10,9... | collective-permute-start | bytes 196616 | tf_op jit(solution)/shard_map/ppermute | solution.py:18
  18.1 5.6 %collective-permute-start.2 = (bf16[2,1,128,128]{3,2,1,0:T(8,128)(2,1)S(1)}, bf16[2,1,128,128]{3,2,1,0:T(8,128)(2,1)S(1)}, u32[]{:S(2)}, u32[]{:S(2)}) collective-permute-start(bf16[2,1,128,128]{3,2,1,0:T(8,128)(2,1)S(1)} %collective-permute-done), channel_id=1, source_target_pairs={{0,1},{1,2},{2,3},{3,4},{4,5},{5,6},{6,7},{7,0},{8,9},{9,10},{10,1... | collective-permute-start | bytes 196616 | tf_op jit(solution)/shard_map/ppermute | solution.py:15
  20.0 9.2 %collective-permute-start.5 = (bf16[2,1,128,128]{3,2,1,0:T(8,128)(2,1)S(1)}, bf16[2,1,128,128]{3,2,1,0:T(8,128)(2,1)S(1)}, u32[]{:S(2)}, u32[]{:S(2)}) collective-permute-start(bf16[2,1,128,128]{3,2,1,0:T(8,128)(2,1)S(1)} %collective-permute-done.3), channel_id=1, source_target_pairs={{0,7},{1,0},{2,1},{3,2},{4,3},{5,4},{6,5},{7,6},{8,15},{9,8},{10,9... | collective-permute-start | bytes 196616 | tf_op jit(solution)/shard_map/ppermute | solution.py:18
  23.8 5.5 %collective-permute-start.4 = (bf16[2,1,128,128]{3,2,1,0:T(8,128)(2,1)S(1)}, bf16[2,1,128,128]{3,2,1,0:T(8,128)(2,1)S(1)}, u32[]{:S(2)}, u32[]{:S(2)}) collective-permute-start(bf16[2,1,128,128]{3,2,1,0:T(8,128)(2,1)S(1)} %collective-permute-done.2), channel_id=1, source_target_pairs={{0,1},{1,2},{2,3},{3,4},{4,5},{5,6},{6,7},{7,0},{8,9},{9,10},{10,1... | collective-permute-start | bytes 196616 | tf_op jit(solution)/shard_map/ppermute | solution.py:15
  29.3 5.5 %collective-permute-start.6 = (bf16[2,1,128,128]{3,2,1,0:T(8,128)(2,1)S(1)}, bf16[2,1,128,128]{3,2,1,0:T(8,128)(2,1)S(1)}, u32[]{:S(2)}, u32[]{:S(2)}) collective-permute-start(bf16[2,1,128,128]{3,2,1,0:T(8,128)(2,1)S(1)} %collective-permute-done.4), channel_id=1, source_target_pairs={{0,1},{1,2},{2,3},{3,4},{4,5},{5,6},{6,7},{7,0},{8,9},{9,10},{10,1... | collective-permute-start | bytes 196616 | tf_op jit(solution)/shard_map/ppermute | solution.py:15
  36.1 0.9 copy-start.4
  36.1 171.3 %all-reduce.9.cloned.1.call-start = ((), (), s32[]{:S(2)}) async-start(), calls=%async_computation.1 | async-start | bytes 524288 | tf_op jit(solution)/shard_map/psum | solution.py:67
  79.2 83.6 %copy-start.1 = (bf16[8,128,128]{1,2,0:T(8,128)(2,1)S(1)}, bf16[8,128,128]{1,2,0:T(8,128)(2,1)}, u32[]{:S(2)}) copy-start(bf16[8,128,128]{1,2,0:T(8,128)(2,1)} %all-reduce.7.cloned.1.call-done) | copy-start | bytes 786436
  164.3 173.1 %all-reduce.11.cloned.1.call-start = ((), (), s32[]{:S(2)}) async-start(), calls=%async_computation.2 | async-start | bytes 524288 | tf_op jit(solution)/shard_map/psum | solution.py:67
  209.2 83.6 %copy-start.3 = (bf16[8,128,128]{1,2,0:T(8,128)(2,1)S(1)}, bf16[8,128,128]{1,2,0:T(8,128)(2,1)}, u32[]{:S(2)}) copy-start(bf16[8,128,128]{1,2,0:T(8,128)(2,1)} %all-reduce.9.cloned.1.call-done) | copy-start | bytes 786436
  339.3 83.6 %copy-start.2 = (bf16[8,128,128]{1,2,0:T(8,128)(2,1)S(1)}, bf16[8,128,128]{1,2,0:T(8,128)(2,1)}, u32[]{:S(2)}) copy-start(bf16[8,128,128]{1,2,0:T(8,128)(2,1)} %all-reduce.11.cloned.1.call-done) | copy-start | bytes 786436
Sparse Core Ops, SparseCore 0:
  36.2 41.1 all-reduce.6
  164.5 42.9 all-reduce.8
  294.5 42.9 all-reduce.10
